TPU v7x, 32 devices: a whole 2x2x4 slice. The times are simulated.
32 devices in a mesh: tensor: 4 (over z), dp: 4 (over y, x), replica: 2 (over core).
Axes of the slice: x: 2, y: 2, z: 4, core: 2. Of those that a mesh axis runs over, the one named last changes fastest.
Arguments:
- states: bfloat16 [8, 256, 4096], P(('dp', 'replica')), may hold values from -6 to 6
- norm_gain: float32 [4096], replicated, may hold values from 0.26 to 4.4
- gate_up: bfloat16 [4096, 2, 14336], P('replica', None, 'tensor'), may hold values from -0.09375 to 0.09375
- cotangent: bfloat16 [8, 256, 14336], P(('dp', 'replica'), None, 'tensor'), may hold values from -120 to 120
- prompt: bfloat16 [32, 4096], replicated, may hold values from -6 to 6
- step_sizes: float32 [3], replicated, may hold values from 0.3 to 1
- insert_at: int32 [8], P(('dp', 'replica')), may hold values from 0 to 224, as said below
- lengths: int32 [8], P(('dp', 'replica')), may hold values from 128 to 256, as said below
Outputs:
- prompt_final: float32 [32, 4096], P(None, 'tensor')
- weight_step: bfloat16 [4096, 2, 14336], P(('dp', 'replica'), None, 'tensor')
Inputs may be any that keep to these rules, and one draw needn't show every extreme that they name: Each prompt lies inside its sequence: insert_at[b] + 32 <= lengths[b]; in every draw some prompt begins at row 0 and some prompt ends at the last row 255. `lengths`: in every draw some sequence has all 256 rows live and some has 128.
All inputs are finite; a program needn't handle non-finite values.
Results may differ from a plain program's by a relative error of at most 0.012.
Values may be sent and summed in bfloat16 or wider, within the bound.
A program may use at most 320 MiB of HBM per device.

v0:
```python
import jax
import jax.numpy as jnp
from jax import lax
from jax.sharding import PartitionSpec as P

D = 4096
FF = 14336


def row_scale(feature_rows):
    return lax.rsqrt(jnp.mean(feature_rows * feature_rows, axis=-1, keepdims=True) + 1e-05)


def silu_parts(gate_values):
    sigmoid_value = jax.nn.sigmoid(gate_values)
    return (
        gate_values * sigmoid_value,
        sigmoid_value * (1.0 + gate_values * (1.0 - sigmoid_value)),
    )


def hidden_grads(normalized, weight_pair, cotan_rows):
    unit_count = weight_pair.shape[1] // 2
    projected = jnp.dot(normalized, weight_pair, preferred_element_type=jnp.float32)
    activated, derivative = silu_parts(projected[:, :unit_count])
    up_part = projected[:, unit_count:]
    return jnp.concatenate(
        [cotan_rows * up_part * derivative, cotan_rows * activated], axis=1
    ).astype(jnp.bfloat16)


def norm_back(shifted, inverse_rms, norm_gain, feature_grad):
    feature_mean = jnp.mean(shifted * norm_gain * feature_grad, axis=-1, keepdims=True)
    return (
        inverse_rms * norm_gain * feature_grad
        - shifted * (inverse_rms * inverse_rms * inverse_rms) * feature_mean
    )


def per_device(states, norm_gain, gate_up, cotangent, prompt, step_sizes, insert_at, lengths):
    gathered = lax.all_gather(gate_up, "replica", axis=0, tiled=True)
    feature_count = gathered.shape[0]
    unit_count = gathered.shape[2]
    weight_pair = gathered.reshape(feature_count, 2 * unit_count)
    seq_states = states[0]
    seq_cotan = cotangent[0].astype(jnp.float32)
    prompt_start = insert_at[0]
    seq_length = lengths[0]
    prompt_count = prompt.shape[0]
    prompt_base = lax.dynamic_slice_in_dim(seq_states, prompt_start, prompt_count, 0).astype(
        jnp.float32
    )
    prompt_cotan = lax.dynamic_slice_in_dim(seq_cotan, prompt_start, prompt_count, 0)
    adversary = prompt.astype(jnp.float32)
    for attack_step in range(step_sizes.shape[0]):
        shifted = prompt_base + adversary
        inverse_rms = row_scale(shifted)
        normalized = (shifted * inverse_rms * norm_gain).astype(jnp.bfloat16)
        unit_grads = hidden_grads(normalized, weight_pair, prompt_cotan)
        feature_grad = lax.dot_general(
            unit_grads, weight_pair, (((1,), (1,)), ((), ())), preferred_element_type=jnp.float32
        )
        feature_grad = lax.psum(feature_grad, "tensor")
        summed_grad = lax.psum(
            norm_back(shifted, inverse_rms, norm_gain, feature_grad), ("dp", "replica")
        )
        adversary = adversary + step_sizes[attack_step] * summed_grad * lax.rsqrt(
            jnp.mean(summed_grad * summed_grad, axis=-1, keepdims=True) + 1e-06
        )
    full_rows = lax.dynamic_update_slice_in_dim(
        seq_states.astype(jnp.float32), prompt_base + adversary, prompt_start, 0
    )
    full_normed = (full_rows * row_scale(full_rows) * norm_gain).astype(jnp.bfloat16)
    positions = lax.broadcasted_iota(jnp.int32, (full_rows.shape[0], 1), 0)
    live_cotan = jnp.where(positions < seq_length, seq_cotan, 0.0)
    token_grads = hidden_grads(full_normed, weight_pair, live_cotan)
    received = lax.all_to_all(
        full_normed, ("dp", "replica"), split_axis=1, concat_axis=0, tiled=True
    )
    weight_grad = lax.dot_general(
        received,
        lax.all_gather(token_grads, ("dp", "replica"), axis=0, tiled=True),
        (((0,), (0,)), ((), ())),
        preferred_element_type=jnp.float32,
    )
    squares = lax.psum(jnp.sum(weight_grad * weight_grad), ("tensor", "dp", "replica"))
    weight_step = (weight_grad * lax.rsqrt(squares / (2 * D * FF) + 1e-06)).astype(jnp.bfloat16)
    weight_step = weight_step.reshape(weight_grad.shape[0], 2, unit_count)
    column_count = adversary.shape[1] // lax.axis_size("tensor")
    prompt_final = lax.dynamic_slice_in_dim(
        adversary, lax.axis_index("tensor") * column_count, column_count, 1
    )
    return (prompt_final, weight_step)


def solution(mesh):
    return jax.shard_map(
        per_device,
        mesh=mesh,
        in_specs=(
            P(("dp", "replica"), None, None),
            P(),
            P("replica", None, "tensor"),
            P(("dp", "replica"), None, "tensor"),
            P(),
            P(),
            P(("dp", "replica")),
            P(("dp", "replica")),
        ),
        out_specs=(P(None, "tensor"), P(("dp", "replica"), None, "tensor")),
        check_vma=False,
    )
```

profile of v0, /device:TPU:0, one launch (start us, length us, event | category | flops | bytes accessed | tf_op | source)
XLA Modules:
  0.0 889.3 jit_solution(5123396470353676943)
XLA Ops:
  8.8 3.8 convert_element_type.43
  12.8 83.6 %all-gather.3.cloned.1.call-done = bf16[4096,2,3584]{2,1,0:T(2,128)(2,1)} async-done(((bf16[2048,2,3584]{2,1,0:T(2,128)(2,1)}), bf16[4096,2,3584]{2,1,0:T(2,128)(2,1)}) %all-gather.3.cloned.1.call-update) | async-done | bytes 58720272 | tf_op jit(solution)/shard_map/all_gather | solution.py:41
  96.4 39.3 %copy.16 = bf16[512,8,2,3584]{3,1,2,0:T(8,128)(2,1)} copy(bf16[512,8,2,3584]{3,2,1,0:T(2,128)(2,1)} %bitcast.75) | data formatting | bytes 117440512
  135.7 21.5 %fusion.23 = f32[32,7168]{1,0:T(8,128)S(1)} fusion(bf16[4096,7168]{1,0:T(8,128)(2,1)} %bitcast.68, bf16[32,4096]{1,0:T(8,128)(2,1)S(1)} %copy-done.2, f32[4096]{0:T(1024)S(1)} %copy-done.5, f32[32]{0:T(128)S(1)} %get-tuple-element.24, bf16[1,256,4096]{2,1,0:T(8,128)(2,1)S(1)} %copy-done.1, s32[]{:T(128)S(6)} %select_n.12), kind=kOutput, calls=%fused_computation.64 | convolution fusion | flops 1879834624 | bytes 60178948 | tf_op jit(solution)/shard_map/dot_general | solution.py:24
  158.5 24.7 %fusion.8 = f32[32,4096]{1,0:T(8,128)} fusion(bf16[4096,7168]{1,0:T(8,128)(2,1)} %bitcast.69, bf16[32,3584]{1,0:T(8,128)(2,1)S(1)} %get-tuple-element.15, bf16[32,3584]{1,0:T(8,128)(2,1)S(1)} %get-tuple-element.14), kind=kOutput, calls=%fused_computation.43 | convolution fusion | flops 1879965696 | bytes 59703296 | tf_op jit(solution)/shard_map/dot_general | solution.py:60
  183.3 39.6 %all-reduce.7.cloned.1.call-done = f32[32,4096]{1,0:T(8,128)} async-done(((f32[32,4096]{1,0:T(8,128)}), f32[32,4096]{1,0:T(8,128)}) %all-reduce.7.cloned.1.call-update) | async-done | bytes 524304 | tf_op jit(solution)/shard_map/psum | solution.py:63
  226.9 54.0 %all-reduce.9.cloned.1.call-done = f32[32,4096]{1,0:T(8,128)} async-done(((f32[32,4096]{1,0:T(8,128)}), f32[32,4096]{1,0:T(8,128)}) %all-reduce.9.cloned.1.call-update) | async-done | bytes 524304 | tf_op jit(solution)/shard_map/psum | solution.py:64
  284.0 21.5 %fusion.24 = f32[32,7168]{1,0:T(8,128)S(1)} fusion(bf16[4096,7168]{1,0:T(8,128)(2,1)} %bitcast.70, f32[32,4096]{1,0:T(8,128)S(1)} %get-tuple-element.7, f32[32]{0:T(128)S(1)} %get-tuple-element.22, f32[4096]{0:T(1024)S(1)} %copy-done.5), kind=kOutput, calls=%fused_computation.65 | convolution fusion | flops 1879441408 | bytes 60178560 | tf_op jit(solution)/shard_map/dot_general | solution.py:24
  306.9 24.7 %fusion.12 = f32[32,4096]{1,0:T(8,128)} fusion(bf16[4096,7168]{1,0:T(8,128)(2,1)} %bitcast.71, bf16[32,3584]{1,0:T(8,128)(2,1)S(1)} %get-tuple-element.13, bf16[32,3584]{1,0:T(8,128)(2,1)S(1)} %get-tuple-element.12), kind=kOutput, calls=%fused_computation.47 | convolution fusion | flops 1879965696 | bytes 59703296 | tf_op jit(solution)/shard_map/dot_general | solution.py:60
  331.6 37.7 %all-reduce.11.cloned.1.call-done = f32[32,4096]{1,0:T(8,128)} async-done(((f32[32,4096]{1,0:T(8,128)}), f32[32,4096]{1,0:T(8,128)}) %all-reduce.11.cloned.1.call-update) | async-done | bytes 524304 | tf_op jit(solution)/shard_map/psum | solution.py:63
  372.9 54.4 %all-reduce.13.cloned.1.call-done = f32[32,4096]{1,0:T(8,128)} async-done(((f32[32,4096]{1,0:T(8,128)}), f32[32,4096]{1,0:T(8,128)}) %all-reduce.13.cloned.1.call-update) | async-done | bytes 524304 | tf_op jit(solution)/shard_map/psum | solution.py:64
  428.5 2.6 multiply_reduce_fusion.4
  431.1 21.4 %fusion.25 = f32[32,7168]{1,0:T(8,128)S(1)} fusion(bf16[4096,7168]{1,0:T(8,128)(2,1)} %bitcast.72, f32[32]{0:T(128)S(1)} %get-tuple-element.20, f32[4096]{0:T(1024)S(1)} %copy-done.5, f32[32,4096]{1,0:T(8,128)S(1)} %get-tuple-element.5, bf16[1,256,4096]{2,1,0:T(8,128)(2,1)S(1)} %copy-done.1, s32[]{:T(128)S(6)} %select_n.12), kind=kOutput, calls=%fused_computation.66 | convolution fusion | flops 1879703552 | bytes 60441092 | tf_op jit(solution)/shard_map/dot_general | solution.py:24
  453.8 24.7 %fusion.16 = f32[32,4096]{1,0:T(8,128)} fusion(bf16[4096,7168]{1,0:T(8,128)(2,1)} %bitcast.73, bf16[32,3584]{1,0:T(8,128)(2,1)S(1)} %get-tuple-element.11, bf16[32,3584]{1,0:T(8,128)(2,1)S(1)} %get-tuple-element.10), kind=kOutput, calls=%fused_computation.51 | convolution fusion | flops 1879965696 | bytes 59703296 | tf_op jit(solution)/shard_map/dot_general | solution.py:60
  478.6 2.5 copy.13
  481.1 35.2 %all-reduce.15.cloned.1.call-done = f32[32,4096]{1,0:T(8,128)} async-done(((f32[32,4096]{1,0:T(8,128)}), f32[32,4096]{1,0:T(8,128)}) %all-reduce.15.cloned.1.call-update) | async-done | bytes 524304 | tf_op jit(solution)/shard_map/psum | solution.py:63
  520.2 3.9 bitcast_convert_fusion
  524.8 49.5 %all-reduce.17.cloned.1.call-done = f32[32,4096]{1,0:T(8,128)} async-done(((f32[32,4096]{1,0:T(8,128)}), f32[32,4096]{1,0:T(8,128)}) %all-reduce.17.cloned.1.call-update) | async-done | bytes 524304 | tf_op jit(solution)/shard_map/psum | solution.py:64
  575.5 2.7 convert_add_fusion
  578.8 11.9 %dynamic_update_slice.3 = f32[256,4096]{0,1:T(8,128)} dynamic-update-slice(f32[256,4096]{0,1:T(8,128)} %bitcast_convert_fusion, f32[32,4096]{0,1:T(8,128)S(1)} %copy.14, s32[]{:T(128)S(6)} %select_n.12, s32[]{:T(128)} %constant.15.clone.1) | dynamic-update-slice | bytes 1048580 | tf_op jit(solution)/shard_map/dynamic_update_slice | solution.py:70
  590.7 2.9 multiply_reduce_fusion.1
  595.9 28.3 %fusion.39 = f32[256,7168]{1,0:T(8,128)} fusion(bf16[256,4096]{0,1:T(8,128)(2,1)} %multiply_convert_fusion.1, bf16[4096,7168]{1,0:T(8,128)(2,1)} %bitcast.74), kind=kOutput, calls=%fused_computation.95 | convolution fusion | flops 15032385536 | bytes 68157440 | tf_op jit(solution)/shard_map/dot_general | solution.py:24
  624.2 4.1 fusion.1
  628.3 2.3 pad_maximum_fusion
  630.6 3.8 all-to-all-start
  636.0 41.6 %all-to-all-done = bf16[256,8,512]{0,2,1:T(8,128)(2,1)S(1)} async-done(((bf16[256,8,512]{0,2,1:T(8,128)(2,1)}), bf16[256,8,512]{0,2,1:T(8,128)(2,1)S(1)}, u32[]{:S(2)}, u32[]{:S(2)}) %all-to-all-start) | async-done | bytes 2097184 | tf_op jit(solution)/shard_map/all_to_all | solution.py:77
  677.6 2.4 copy.15
  680.0 109.1 %all-gather.5.cloned.1.call-done = bf16[2048,7168]{1,0:T(8,128)(2,1)} async-done(((bf16[256,7168]{1,0:T(8,128)(2,1)}), bf16[2048,7168]{1,0:T(8,128)(2,1)}) %all-gather.5.cloned.1.call-update) | async-done | bytes 29360144 | tf_op jit(solution)/shard_map/all_gather | solution.py:82
  789.1 26.1 %multiply_reduce_fusion = (f32[]{:T(128)}, f32[512,7168]{1,0:T(8,128)}) fusion(bf16[2048,512]{1,0:T(8,128)(2,1)} %bitcast.77, bf16[2048,7168]{1,0:T(8,128)(2,1)} %all-gather.5.cloned.1.call-done), kind=kOutput, calls=%fused_computation.1 | convolution fusion | flops 15039725568 | bytes 46137348 | tf_op jit(solution)/shard_map/dot_general | solution.py:80
  815.2 39.7 %psum.55 = f32[]{:T(128)} all-reduce(f32[]{:T(128)} %get-tuple-element.25), channel_id=1, replica_groups=mesh['tensor'=4,'dp'=4,'replica'=2] {'tensor','dp','replica'}, use_global_device_ids=true, to_apply=%region_17.18 | all-reduce | flops 1 | bytes 8 | tf_op jit(solution)/shard_map/psum | solution.py:86
  855.6 9.8 %multiply_convert_fusion = bf16[512,7168]{1,0:T(8,128)(2,1)} fusion(f32[512,7168]{1,0:T(8,128)} %get-tuple-element.26, f32[]{:T(128)S(6)} %rsqrt.75), kind=kLoop, calls=%fused_computation | loop fusion | flops 7340032 | bytes 22020100 | tf_op jit(solution)/shard_map/convert_element_type | solution.py:87
  865.4 16.9 %reshape.113 = bf16[512,2,3584]{2,1,0:T(2,128)(2,1)} reshape(bf16[512,7168]{1,0:T(8,128)(2,1)} %multiply_convert_fusion) | data formatting | bytes 14680064 | tf_op jit(solution)/shard_map/reshape | solution.py:88
  (59 shorter events, 26.6 us)
Async XLA Ops:
  7.2 89.3 %all-gather.3.cloned.1.call-start = ((), (), s32[]{:S(2)}) async-start(), calls=%async_computation.1 | async-start | bytes 88080384 | tf_op jit(solution)/shard_map/all_gather | solution.py:41
  7.9 4.6 copy-start.1
  7.9 4.6 copy-start.2
  7.9 214.9 %all-reduce.7.cloned.1.call-start = ((), (), s32[]{:S(2)}) async-start(), calls=%async_computation.2 | async-start | bytes 1048576 | tf_op jit(solution)/shard_map/psum | solution.py:63
  96.4 39.3 %copy-start.5 = (f32[4096]{0:T(1024)S(1)}, f32[4096]{0:T(1024)}, u32[]{:S(2)}) copy-start(f32[4096]{0:T(1024)} %param.9) | copy-start | bytes 49156
  183.2 43.0 %copy-start.6 = (f32[3]{0:T(128)S(1)}, f32[3]{0:T(128)}, u32[]{:S(2)}) copy-start(f32[3]{0:T(128)} %param.13) | copy-start | bytes 40
  183.3 97.6 %all-reduce.9.cloned.1.call-start = ((), (), s32[]{:S(2)}) async-start(), calls=%async_computation.3 | async-start | bytes 1048576 | tf_op jit(solution)/shard_map/psum | solution.py:64
  226.2 143.1 %all-reduce.11.cloned.1.call-start = ((), (), s32[]{:S(2)}) async-start(), calls=%async_computation.4 | async-start | bytes 1048576 | tf_op jit(solution)/shard_map/psum | solution.py:63
  331.5 96.9 %copy-start.4 = (f32[32,4096]{1,0:T(8,128)S(1)}, f32[32,4096]{1,0:T(8,128)}, u32[]{:S(2)}) copy-start(f32[32,4096]{1,0:T(8,128)} %all-reduce.9.cloned.1.call-done) | copy-start | bytes 1572868
  331.6 95.7 %all-reduce.13.cloned.1.call-start = ((), (), s32[]{:S(2)}) async-start(), calls=%async_computation.5 | async-start | bytes 1048576 | tf_op jit(solution)/shard_map/psum | solution.py:64
  372.6 143.8 %all-reduce.15.cloned.1.call-start = ((), (), s32[]{:S(2)}) async-start(), calls=%async_computation.6 | async-start | bytes 1048576 | tf_op jit(solution)/shard_map/psum | solution.py:63
  478.6 95.8 %all-reduce.17.cloned.1.call-start = ((), (), s32[]{:S(2)}) async-start(), calls=%async_computation.7 | async-start | bytes 1048576 | tf_op jit(solution)/shard_map/psum | solution.py:64
  519.6 269.4 %all-gather.5.cloned.1.call-start = ((), (), s32[]{:S(2)}) async-start(), calls=%async_computation.8 | async-start | bytes 33030144 | tf_op jit(solution)/shard_map/all_gather | solution.py:82
  590.7 3.4 copy-start
  595.9 28.3 %copy-start.3 = (bf16[1,256,3584]{2,1,0:T(8,128)(2,1)S(1)}, bf16[1,256,3584]{2,1,0:T(8,128)(2,1)}, u32[]{:S(2)}) copy-start(bf16[1,256,3584]{2,1,0:T(8,128)(2,1)} %param.11) | copy-start | bytes 5505028
  630.6 47.0 %all-to-all-start = ((bf16[256,8,512]{0,2,1:T(8,128)(2,1)}), bf16[256,8,512]{0,2,1:T(8,128)(2,1)S(1)}, u32[]{:S(2)}, u32[]{:S(2)}) async-start(bf16[256,8,512]{0,2,1:T(8,128)(2,1)} %bitcast.8), calls=%async_computation | async-start | bytes 4194304 | tf_op jit(solution)/shard_map/all_to_all | solution.py:77
Sparse Core Ops, SparseCore 0:
  9.5 86.8 all-gather.2
  183.4 39.4 all-reduce.6
  226.3 54.5 all-reduce.8
  331.7 37.5 all-reduce.10
  372.7 54.5 all-reduce.12
  478.7 37.5 all-reduce.14
  519.8 54.5 all-reduce.16
  630.7 158.2 all-gather.4
where the time goes:
time: 900 us; the launch traced here: 889 us
  waiting for transfers between devices  505 us (56%)
  matrix products  193 us (21%)
  local copies, waits for them, and re-layouts  76.3 us (8%)
  other arithmetic  53.3 us (6%)
  blocking collectives  39.7 us (4%)
  between operations  16.6 us (2%)
    psum x3, waiting for transfers between devices, per_device(): lax.psum(norm_back(shifted, inverse_rms, norm_gain, feature_grad), ('dp',...  158 us
    psum x3, waiting for transfers between devices, per_device(): feature_grad = lax.psum(feature_grad, 'tensor')  112 us
    all_gather x1, waiting for transfers between devices, per_device(): lax.all_gather(token_grads, ('dp', 'replica'), axis=0, tiled=True)  109 us
    dot_general x4, matrix products, hidden_grads(): jnp.dot(normalized, weight_pair, preferred_element_type=jnp.float32)  92.8 us
    all_gather x1, waiting for transfers between devices, per_device(): gathered = lax.all_gather(gate_up, 'replica', axis=0, tiled=True)  83.6 us
    dot_general x3, matrix products, per_device(): lax.dot_general(unit_grads, weight_pair, (((1,), (1,)), ((), ())), prefer...  74.1 us
    unnamed x16, local copies, waits for them, and re-layouts  42.3 us
    all_to_all x1, waiting for transfers between devices, per_device(): lax.all_to_all(full_normed, ('dp', 'replica'), split_axis=1, concat_axis=...  41.6 us
  transfers between devices with their start and end apart: 9, of which 9 were waited for; matrix products, arithmetic and copies ran while one was open for 2% of the time, Pallas kernels for 0%

commit v1 on v0

--- a/solution.py
+++ b/solution.py
@@ -61,9 +61,9 @@
             unit_grads, weight_pair, (((1,), (1,)), ((), ())), preferred_element_type=jnp.float32
         )
         feature_grad = lax.psum(feature_grad, "tensor")
-        summed_grad = lax.psum(
-            norm_back(shifted, inverse_rms, norm_gain, feature_grad), ("dp", "replica")
-        )
+        summed_grad = norm_back(shifted, inverse_rms, norm_gain, feature_grad)
+        for over in ("replica", "dp"):
+            summed_grad = lax.psum(summed_grad, over)
         adversary = adversary + step_sizes[attack_step] * summed_grad * lax.rsqrt(
             jnp.mean(summed_grad * summed_grad, axis=-1, keepdims=True) + 1e-06
         )

time: 900 us -> 942 us (1.047)
  waiting for transfers between devices: 505 us -> 548 us
    psum x3 -> x6, waiting for transfers between devices: 158 us -> 197 us  [per_device(): summed_grad = lax.psum(summed_grad, over)]
  transfers between devices with their start and end apart: 9 -> 12, of which waited for: 9 -> 12; matrix products, arithmetic and copies ran while one was open for 2% -> 2% of each run, Pallas kernels for 0% -> 0%
where the time goes in v1:
time: 942 us; the launch traced here: 932 us
  waiting for transfers between devices  548 us (58%)
  matrix products  193 us (20%)
  local copies, waits for them, and re-layouts  76.3 us (8%)
  other arithmetic  53.4 us (6%)
  blocking collectives  39.7 us (4%)
  between operations  16.4 us (2%)
    psum x6, waiting for transfers between devices, per_device(): summed_grad = lax.psum(summed_grad, over)  197 us
    psum x3, waiting for transfers between devices, per_device(): feature_grad = lax.psum(feature_grad, 'tensor')  116 us
    all_gather x1, waiting for transfers between devices, per_device(): lax.all_gather(token_grads, ('dp', 'replica'), axis=0, tiled=True)  110 us
    dot_general x4, matrix products, hidden_grads(): jnp.dot(normalized, weight_pair, preferred_element_type=jnp.float32)  92.8 us
    all_gather x1, waiting for transfers between devices, per_device(): gathered = lax.all_gather(gate_up, 'replica', axis=0, tiled=True)  83.6 us
    dot_general x3, matrix products, per_device(): lax.dot_general(unit_grads, weight_pair, (((1,), (1,)), ((), ())), prefer...  74.1 us
    unnamed x16, local copies, waits for them, and re-layouts  42.3 us
    all_to_all x1, waiting for transfers between devices, per_device(): lax.all_to_all(full_normed, ('dp', 'replica'), split_axis=1, concat_axis=...  41 us
  transfers between devices with their start and end apart: 12, of which 12 were waited for; matrix products, arithmetic and copies ran while one was open for 2% of the time, Pallas kernels for 0%

profile of v1, /device:TPU:0, one launch (start us, length us, event | category | flops | bytes accessed | tf_op | source)
XLA Modules:
  0.0 932.1 jit_solution(11572833854644070070)
XLA Ops:
  8.8 3.8 convert_element_type.43
  12.8 83.6 %all-gather.3.cloned.1.call-done = bf16[4096,2,3584]{2,1,0:T(2,128)(2,1)} async-done(((bf16[2048,2,3584]{2,1,0:T(2,128)(2,1)}), bf16[4096,2,3584]{2,1,0:T(2,128)(2,1)}) %all-gather.3.cloned.1.call-update) | async-done | bytes 58720272 | tf_op jit(solution)/shard_map/all_gather | solution.py:41
  96.4 39.3 %copy.16 = bf16[512,8,2,3584]{3,1,2,0:T(8,128)(2,1)} copy(bf16[512,8,2,3584]{3,2,1,0:T(2,128)(2,1)} %bitcast.75) | data formatting | bytes 117440512
  135.7 21.5 %fusion.23 = f32[32,7168]{1,0:T(8,128)S(1)} fusion(bf16[4096,7168]{1,0:T(8,128)(2,1)} %bitcast.68, bf16[32,4096]{1,0:T(8,128)(2,1)S(1)} %copy-done.2, f32[4096]{0:T(1024)S(1)} %copy-done.5, f32[32]{0:T(128)S(1)} %get-tuple-element.24, bf16[1,256,4096]{2,1,0:T(8,128)(2,1)S(1)} %copy-done.1, s32[]{:T(128)S(6)} %select_n.12), kind=kOutput, calls=%fused_computation.64 | convolution fusion | flops 1879834624 | bytes 60178948 | tf_op jit(solution)/shard_map/dot_general | solution.py:24
  158.5 24.7 %fusion.8 = f32[32,4096]{1,0:T(8,128)} fusion(bf16[4096,7168]{1,0:T(8,128)(2,1)} %bitcast.69, bf16[32,3584]{1,0:T(8,128)(2,1)S(1)} %get-tuple-element.15, bf16[32,3584]{1,0:T(8,128)(2,1)S(1)} %get-tuple-element.14), kind=kOutput, calls=%fused_computation.43 | convolution fusion | flops 1879965696 | bytes 59703296 | tf_op jit(solution)/shard_map/dot_general | solution.py:60
  183.3 39.6 %all-reduce.10.cloned.1.call-done = f32[32,4096]{1,0:T(8,128)} async-done(((f32[32,4096]{1,0:T(8,128)}), f32[32,4096]{1,0:T(8,128)}) %all-reduce.10.cloned.1.call-update) | async-done | bytes 524304 | tf_op jit(solution)/shard_map/psum | solution.py:63
  226.3 18.8 %all-reduce.12.cloned.1.call-done = f32[32,4096]{1,0:T(8,128)} async-done(((f32[32,4096]{1,0:T(8,128)}), f32[32,4096]{1,0:T(8,128)}) %all-reduce.12.cloned.1.call-update) | async-done | bytes 524304 | tf_op jit(solution)/shard_map/psum | solution.py:66
  245.8 49.0 %all-reduce.14.cloned.1.call-done = f32[32,4096]{1,0:T(8,128)} async-done(((f32[32,4096]{1,0:T(8,128)}), f32[32,4096]{1,0:T(8,128)}) %all-reduce.14.cloned.1.call-update) | async-done | bytes 524304 | tf_op jit(solution)/shard_map/psum | solution.py:66
  298.0 21.5 %fusion.24 = f32[32,7168]{1,0:T(8,128)S(1)} fusion(bf16[4096,7168]{1,0:T(8,128)(2,1)} %bitcast.70, f32[32,4096]{1,0:T(8,128)S(1)} %get-tuple-element.7, f32[32]{0:T(128)S(1)} %get-tuple-element.22, f32[4096]{0:T(1024)S(1)} %copy-done.5), kind=kOutput, calls=%fused_computation.65 | convolution fusion | flops 1879441408 | bytes 60178560 | tf_op jit(solution)/shard_map/dot_general | solution.py:24
  320.8 24.7 %fusion.12 = f32[32,4096]{1,0:T(8,128)} fusion(bf16[4096,7168]{1,0:T(8,128)(2,1)} %bitcast.71, bf16[32,3584]{1,0:T(8,128)(2,1)S(1)} %get-tuple-element.13, bf16[32,3584]{1,0:T(8,128)(2,1)S(1)} %get-tuple-element.12), kind=kOutput, calls=%fused_computation.47 | convolution fusion | flops 1879965696 | bytes 59703296 | tf_op jit(solution)/shard_map/dot_general | solution.py:60
  345.6 38.4 %all-reduce.16.cloned.1.call-done = f32[32,4096]{1,0:T(8,128)} async-done(((f32[32,4096]{1,0:T(8,128)}), f32[32,4096]{1,0:T(8,128)}) %all-reduce.16.cloned.1.call-update) | async-done | bytes 524304 | tf_op jit(solution)/shard_map/psum | solution.py:63
  387.3 18.8 %all-reduce.18.cloned.1.call-done = f32[32,4096]{1,0:T(8,128)} async-done(((f32[32,4096]{1,0:T(8,128)}), f32[32,4096]{1,0:T(8,128)}) %all-reduce.18.cloned.1.call-update) | async-done | bytes 524304 | tf_op jit(solution)/shard_map/psum | solution.py:66
  406.5 49.2 %all-reduce.20.cloned.1.call-done = f32[32,4096]{1,0:T(8,128)} async-done(((f32[32,4096]{1,0:T(8,128)}), f32[32,4096]{1,0:T(8,128)}) %all-reduce.20.cloned.1.call-update) | async-done | bytes 524304 | tf_op jit(solution)/shard_map/psum | solution.py:66
  456.8 2.7 multiply_reduce_fusion.4
  459.5 21.4 %fusion.25 = f32[32,7168]{1,0:T(8,128)S(1)} fusion(bf16[4096,7168]{1,0:T(8,128)(2,1)} %bitcast.72, f32[32]{0:T(128)S(1)} %get-tuple-element.20, f32[4096]{0:T(1024)S(1)} %copy-done.5, f32[32,4096]{1,0:T(8,128)S(1)} %get-tuple-element.5, bf16[1,256,4096]{2,1,0:T(8,128)(2,1)S(1)} %copy-done.1, s32[]{:T(128)S(6)} %select_n.12), kind=kOutput, calls=%fused_computation.66 | convolution fusion | flops 1879703552 | bytes 60441092 | tf_op jit(solution)/shard_map/dot_general | solution.py:24
  482.3 24.7 %fusion.16 = f32[32,4096]{1,0:T(8,128)} fusion(bf16[4096,7168]{1,0:T(8,128)(2,1)} %bitcast.73, bf16[32,3584]{1,0:T(8,128)(2,1)S(1)} %get-tuple-element.11, bf16[32,3584]{1,0:T(8,128)(2,1)S(1)} %get-tuple-element.10), kind=kOutput, calls=%fused_computation.51 | convolution fusion | flops 1879965696 | bytes 59703296 | tf_op jit(solution)/shard_map/dot_general | solution.py:60
  507.1 38.4 %all-reduce.22.cloned.1.call-done = f32[32,4096]{1,0:T(8,128)} async-done(((f32[32,4096]{1,0:T(8,128)}), f32[32,4096]{1,0:T(8,128)}) %all-reduce.22.cloned.1.call-update) | async-done | bytes 524304 | tf_op jit(solution)/shard_map/psum | solution.py:63
  551.4 16.3 %all-reduce.24.cloned.1.call-done = f32[32,4096]{1,0:T(8,128)} async-done(((f32[32,4096]{1,0:T(8,128)}), f32[32,4096]{1,0:T(8,128)}) %all-reduce.24.cloned.1.call-update) | async-done | bytes 524304 | tf_op jit(solution)/shard_map/psum | solution.py:66
  568.2 3.9 bitcast_convert_fusion
  572.8 44.5 %all-reduce.26.cloned.1.call-done = f32[32,4096]{1,0:T(8,128)} async-done(((f32[32,4096]{1,0:T(8,128)}), f32[32,4096]{1,0:T(8,128)}) %all-reduce.26.cloned.1.call-update) | async-done | bytes 524304 | tf_op jit(solution)/shard_map/psum | solution.py:66
  618.5 2.7 convert_add_fusion
  621.8 11.9 %dynamic_update_slice.3 = f32[256,4096]{0,1:T(8,128)} dynamic-update-slice(f32[256,4096]{0,1:T(8,128)} %bitcast_convert_fusion, f32[32,4096]{0,1:T(8,128)S(1)} %copy.14, s32[]{:T(128)S(6)} %select_n.12, s32[]{:T(128)} %constant.15.clone.1) | dynamic-update-slice | bytes 1048580 | tf_op jit(solution)/shard_map/dynamic_update_slice | solution.py:70
  633.7 2.9 multiply_reduce_fusion.1
  638.9 28.3 %fusion.39 = f32[256,7168]{1,0:T(8,128)} fusion(bf16[256,4096]{0,1:T(8,128)(2,1)} %multiply_convert_fusion.1, bf16[4096,7168]{1,0:T(8,128)(2,1)} %bitcast.74), kind=kOutput, calls=%fused_computation.95 | convolution fusion | flops 15032385536 | bytes 68157440 | tf_op jit(solution)/shard_map/dot_general | solution.py:24
  667.2 4.1 fusion.1
  673.6 3.8 all-to-all-start
  679.0 41.0 %all-to-all-done = bf16[256,8,512]{0,2,1:T(8,128)(2,1)S(1)} async-done(((bf16[256,8,512]{0,2,1:T(8,128)(2,1)}), bf16[256,8,512]{0,2,1:T(8,128)(2,1)S(1)}, u32[]{:S(2)}, u32[]{:S(2)}) %all-to-all-start) | async-done | bytes 2097184 | tf_op jit(solution)/shard_map/all_to_all | solution.py:77
  722.3 109.8 %all-gather.5.cloned.1.call-done = bf16[2048,7168]{1,0:T(8,128)(2,1)} async-done(((bf16[256,7168]{1,0:T(8,128)(2,1)}), bf16[2048,7168]{1,0:T(8,128)(2,1)}) %all-gather.5.cloned.1.call-update) | async-done | bytes 29360144 | tf_op jit(solution)/shard_map/all_gather | solution.py:82
  832.1 26.1 %multiply_reduce_fusion = (f32[]{:T(128)}, f32[512,7168]{1,0:T(8,128)}) fusion(bf16[2048,512]{1,0:T(8,128)(2,1)} %bitcast.77, bf16[2048,7168]{1,0:T(8,128)(2,1)} %all-gather.5.cloned.1.call-done), kind=kOutput, calls=%fused_computation.1 | convolution fusion | flops 15039725568 | bytes 46137348 | tf_op jit(solution)/shard_map/dot_general | solution.py:80
  858.3 39.7 %psum.79 = f32[]{:T(128)} all-reduce(f32[]{:T(128)} %get-tuple-element.25), channel_id=1, replica_groups=mesh['tensor'=4,'dp'=4,'replica'=2] {'tensor','dp','replica'}, use_global_device_ids=true, to_apply=%region_20.21 | all-reduce | flops 1 | bytes 8 | tf_op jit(solution)/shard_map/psum | solution.py:86
  898.7 9.8 %multiply_convert_fusion = bf16[512,7168]{1,0:T(8,128)(2,1)} fusion(f32[512,7168]{1,0:T(8,128)} %get-tuple-element.26, f32[]{:T(128)S(6)} %rsqrt.75), kind=kLoop, calls=%fused_computation | loop fusion | flops 7340032 | bytes 22020100 | tf_op jit(solution)/shard_map/convert_element_type | solution.py:87
  908.5 16.9 %reshape.113 = bf16[512,2,3584]{2,1,0:T(2,128)(2,1)} reshape(bf16[512,7168]{1,0:T(8,128)(2,1)} %multiply_convert_fusion) | data formatting | bytes 14680064 | tf_op jit(solution)/shard_map/reshape | solution.py:88
  (68 shorter events, 34.0 us)
Async XLA Ops:
  7.2 89.3 %all-gather.3.cloned.1.call-start = ((), (), s32[]{:S(2)}) async-start(), calls=%async_computation.1 | async-start | bytes 88080384 | tf_op jit(solution)/shard_map/all_gather | solution.py:41
  7.9 4.6 copy-start.1
  7.9 4.6 copy-start.2
  7.9 214.9 %all-reduce.10.cloned.1.call-start = ((), (), s32[]{:S(2)}) async-start(), calls=%async_computation.2 | async-start | bytes 1048576 | tf_op jit(solution)/shard_map/psum | solution.py:63
  96.4 39.3 %copy-start.5 = (f32[4096]{0:T(1024)S(1)}, f32[4096]{0:T(1024)}, u32[]{:S(2)}) copy-start(f32[4096]{0:T(1024)} %param.9) | copy-start | bytes 49156
  183.2 61.9 %copy-start.6 = (f32[3]{0:T(128)S(1)}, f32[3]{0:T(128)}, u32[]{:S(2)}) copy-start(f32[3]{0:T(128)} %param.13) | copy-start | bytes 40
  183.3 61.8 %all-reduce.12.cloned.1.call-start = ((), (), s32[]{:S(2)}) async-start(), calls=%async_computation.3 | async-start | bytes 1048576 | tf_op jit(solution)/shard_map/psum | solution.py:66
  226.2 68.6 %all-reduce.14.cloned.1.call-start = ((), (), s32[]{:S(2)}) async-start(), calls=%async_computation.4 | async-start | bytes 1048576 | tf_op jit(solution)/shard_map/psum | solution.py:66
  245.1 138.9 %all-reduce.16.cloned.1.call-start = ((), (), s32[]{:S(2)}) async-start(), calls=%async_computation.5 | async-start | bytes 1048576 | tf_op jit(solution)/shard_map/psum | solution.py:63
  345.5 111.4 %copy-start.4 = (f32[32,4096]{1,0:T(8,128)S(1)}, f32[32,4096]{1,0:T(8,128)}, u32[]{:S(2)}) copy-start(f32[32,4096]{1,0:T(8,128)} %all-reduce.14.cloned.1.call-done) | copy-start | bytes 1572868
  345.5 60.6 %all-reduce.18.cloned.1.call-start = ((), (), s32[]{:S(2)}) async-start(), calls=%async_computation.6 | async-start | bytes 1048576 | tf_op jit(solution)/shard_map/psum | solution.py:66
  387.2 68.4 %all-reduce.20.cloned.1.call-start = ((), (), s32[]{:S(2)}) async-start(), calls=%async_computation.7 | async-start | bytes 1048576 | tf_op jit(solution)/shard_map/psum | solution.py:66
  406.1 139.3 %all-reduce.22.cloned.1.call-start = ((), (), s32[]{:S(2)}) async-start(), calls=%async_computation.8 | async-start | bytes 1048576 | tf_op jit(solution)/shard_map/psum | solution.py:63
  507.0 60.6 %all-reduce.24.cloned.1.call-start = ((), (), s32[]{:S(2)}) async-start(), calls=%async_computation.9 | async-start | bytes 1048576 | tf_op jit(solution)/shard_map/psum | solution.py:66
  548.8 68.5 %all-reduce.26.cloned.1.call-start = ((), (), s32[]{:S(2)}) async-start(), calls=%async_computation.10 | async-start | bytes 1048576 | tf_op jit(solution)/shard_map/psum | solution.py:66
  567.7 264.5 %all-gather.5.cloned.1.call-start = ((), (), s32[]{:S(2)}) async-start(), calls=%async_computation.11 | async-start | bytes 33030144 | tf_op jit(solution)/shard_map/all_gather | solution.py:82
  633.7 3.4 copy-start
  638.9 28.3 %copy-start.3 = (bf16[1,256,3584]{2,1,0:T(8,128)(2,1)S(1)}, bf16[1,256,3584]{2,1,0:T(8,128)(2,1)}, u32[]{:S(2)}) copy-start(bf16[1,256,3584]{2,1,0:T(8,128)(2,1)} %param.11) | copy-start | bytes 5505028
  673.6 46.3 %all-to-all-start = ((bf16[256,8,512]{0,2,1:T(8,128)(2,1)}), bf16[256,8,512]{0,2,1:T(8,128)(2,1)S(1)}, u32[]{:S(2)}, u32[]{:S(2)}) async-start(bf16[256,8,512]{0,2,1:T(8,128)(2,1)} %bitcast.8), calls=%async_computation | async-start | bytes 4194304 | tf_op jit(solution)/shard_map/all_to_all | solution.py:77
Sparse Core Ops, SparseCore 0:
  9.5 86.8 all-gather.2
  183.4 39.4 all-reduce.9
  226.3 18.6 all-reduce.11
  248.2 46.5 all-reduce.13
  345.6 38.2 all-reduce.15
  387.3 18.7 all-reduce.17
  409.1 46.5 all-reduce.19
  507.2 38.2 all-reduce.21
  548.9 18.6 all-reduce.23
  570.8 46.5 all-reduce.25
  673.7 158.3 all-gather.4
